TPU v7x, 32 devices: a whole 2x2x4 slice. The times are simulated.
32 devices in a mesh: src: 16 (over z, x, core), tgt: 2 (over y).
Axes of the slice: x: 2, y: 2, z: 4, core: 2. Of those that a mesh axis runs over, the one named last changes fastest.
Arguments:
- source_embed: bfloat16 [128, 65536], P(None, 'src'), may hold values from -1 to 1
- target_embed: bfloat16 [128, 1024], P(None, 'tgt'), may hold values from -1 to 1
- source_expr: bfloat16 [128, 65536], P(None, 'src'), may hold values from -0.5390625 to 0.5390625
- target_expr: bfloat16 [128, 1024], P(None, 'tgt'), may hold values from -0.5390625 to 0.5390625
- current_plan: bfloat16 [65536, 1024], P('src', 'tgt'), as said below
- source_mass: float32 [65536], P('src'), may hold values from 0.25 to 4
- target_mass: float32 [1024], P('tgt'), may hold values from 0.25 to 4
- source_potential: float32 [65536], P('src'), may hold values from -16 to 16
- target_genes: bfloat16 [1024, 256], P('tgt'), may hold values from -6 to 6
Outputs:
- imputed: bfloat16 [65536, 256], P(('src', 'tgt'))
Inputs may be any that keep to these rules, and one draw needn't show every extreme that they name: Every entry of current_plan is positive.
All inputs are finite; a program needn't handle non-finite values.
Results may differ from a plain program's by a relative error of at most 0.014.
Values may be sent and summed in bfloat16 or wider, within the bound.
A program may use at most 64 MiB of HBM per device.

v0:
```python
import jax
import jax.numpy as jnp
from jax import lax
from jax.sharding import PartitionSpec as P

ITERS = 2
epsilon = 0.05
geometry_weight = 4.0


def joined(value, axis, join):
    pieces = jax.tree.map(lambda part: lax.all_gather(part, axis), value)
    head = jax.tree.map(lambda part: part[0], pieces)
    tail = jax.tree.map(lambda part: part[1:], pieces)
    so_far, _ = lax.scan(lambda so_far, piece: (join(so_far, piece), None), head, tail)
    return so_far


def factors(embed):
    widened = embed.astype(jnp.float32)
    squares = jnp.sum(widened * widened, axis=0)
    unit_row = jnp.ones_like(squares)
    left_factor = jnp.concatenate([squares[None, :], unit_row[None, :], -2.0 * widened], axis=0)
    right_factor = jnp.concatenate([unit_row[None, :], squares[None, :], widened], axis=0)
    return (left_factor, right_factor)


def combine_pair(earlier, later):
    maximum = jnp.maximum(earlier[0], later[0])
    return (
        maximum,
        earlier[1] * jnp.exp(earlier[0] - maximum) + later[1] * jnp.exp(later[0] - maximum),
    )


def column_logsum(scores):
    local_max = jnp.max(scores, axis=0)
    local_sum = jnp.sum(jnp.exp(scores - local_max[None, :]), axis=0)
    maximum, totals = joined((local_max, local_sum), "src", combine_pair)
    return maximum + jnp.log(totals)


def row_logsum(scores):
    local_max = jnp.max(scores, axis=1)
    local_sum = jnp.sum(jnp.exp(scores - local_max[:, None]), axis=1)
    maximum, totals = joined((local_max, local_sum), "tgt", combine_pair)
    return maximum + jnp.log(totals)


def shards(
    source_embed,
    target_embed,
    source_expr,
    target_expr,
    current_plan,
    source_mass,
    target_mass,
    source_potential,
    target_genes,
):
    highest = lax.Precision.HIGHEST
    spot_rows = source_embed.shape[1]
    spot_cols = target_embed.shape[1]
    total_pairs = float(spot_rows * lax.axis_size("src") * spot_cols * lax.axis_size("tgt"))
    left_src, right_src = factors(source_embed)
    left_tgt, right_tgt = factors(target_embed)
    projected = jnp.dot(
        current_plan.astype(jnp.float32),
        right_tgt.T,
        precision=highest,
        preferred_element_type=jnp.float32,
    )
    partial_core = jnp.dot(
        right_src, projected, precision=highest, preferred_element_type=jnp.float32
    )
    core_matrix = lax.psum(partial_core, ("src", "tgt")) / total_pairs
    geometry_right = jnp.dot(
        core_matrix, left_tgt, precision=highest, preferred_element_type=jnp.float32
    )
    geometry = lax.dot_general(
        left_src,
        geometry_right,
        (((0,), (0,)), ((), ())),
        precision=highest,
        preferred_element_type=jnp.float32,
    )
    feature = lax.dot_general(
        source_expr, target_expr, (((0,), (0,)), ((), ())), preferred_element_type=jnp.float32
    )
    cost_tile = -2.0 * (feature + geometry_weight * geometry)
    log_src = jnp.log(source_mass)
    log_tgt = jnp.log(target_mass)
    potential_src = source_potential
    potential_tgt = jnp.zeros((spot_cols,), jnp.float32)
    for iteration in range(ITERS):
        potential_tgt = epsilon * log_tgt - epsilon * column_logsum(
            (potential_src[:, None] - cost_tile) / epsilon
        )
        potential_src = epsilon * log_src - epsilon * row_logsum(
            (potential_tgt[None, :] - cost_tile) / epsilon
        )
    weights = jnp.exp(
        (potential_src[:, None] + potential_tgt[None, :] - cost_tile) / epsilon
    ).astype(jnp.bfloat16)
    row_share = spot_rows // lax.axis_size("tgt")
    row_offset = lax.axis_index("tgt") * row_share
    mass_rows = lax.dynamic_slice_in_dim(source_mass, row_offset, row_share)
    numerator = lax.psum_scatter(
        jnp.dot(weights, target_genes, preferred_element_type=jnp.float32).astype(jnp.bfloat16),
        "tgt",
        scatter_dimension=0,
        tiled=True,
    ).astype(jnp.float32)
    return (numerator / mass_rows[:, None]).astype(jnp.bfloat16)


def solution(mesh):
    return jax.shard_map(
        shards,
        mesh=mesh,
        in_specs=(
            P(None, "src"),
            P(None, "tgt"),
            P(None, "src"),
            P(None, "tgt"),
            P("src", "tgt"),
            P("src"),
            P("tgt"),
            P("src"),
            P("tgt", None),
        ),
        out_specs=P(("src", "tgt"), None),
        check_vma=False,
    )
```

profile of v0, /device:TPU:0, one launch (start us, length us, event | category | flops | bytes accessed | tf_op | source)
XLA Modules:
  0.0 319.4 jit_solution(5949856165096476949)
XLA Ops:
  6.5 0.0 copy-start
  6.5 0.0 all-reduce.2.cloned.1.call-start
  6.5 0.0 copy-start.3
  6.5 1.1 multiply_reduce_fusion.1
  7.7 1.2 convert_element_type.20
  8.9 1.6 broadcast_multiply_fusion
  10.4 1.4 convert_element_type.19
  11.9 0.0 copy-done.3
  11.9 4.3 %fusion.18 = f32[130,4096]{1,0:T(8,128)S(1)} fusion(bf16[4096,512]{1,0:T(8,128)(2,1)S(1)} %copy-done.3, f32[128,512]{1,0:T(8,128)S(1)} %convert_element_type.20, f32[1,512]{1,0:T(1,128)S(1)} %bitcast.56, f32[1,512]{1,0:T(1,128)S(1)} %broadcast.34), kind=kOutput, calls=%fused_computation.38 | convolution fusion | flops 3271690240 | bytes 6590464 | tf_op jit(solution)/shard_map/dot_general | solution.py:67
  16.2 2.8 fusion.12
  19.0 0.0 copy-start.5
  19.0 0.0 all-reduce.2.cloned.1.call-update
  19.0 0.2 reduce-scatter.2.cloned.1.call-start
  19.3 0.0 copy-done
  19.3 5.4 %fusion.50 = f32[4096,512]{1,0:T(8,128)} fusion(bf16[128,4096]{1,0:T(8,128)(2,1)S(1)} %copy-done, bf16[128,512]{1,0:T(8,128)(2,1)} %param.16), kind=kOutput, calls=%fused_computation.86 | convolution fusion | flops 536870912 | bytes 9568256 | tf_op jit(solution)/shard_map/dot_general | solution.py:87
  24.7 117.4 %all-reduce.2.cloned.1.call-done = f32[130,130]{1,0:T(8,128)} async-done(((f32[130,130]{1,0:T(8,128)}), f32[130,130]{1,0:T(8,128)}) %all-reduce.2.cloned.1.call-update) | async-done | bytes 67616 | tf_op jit(solution)/shard_map/psum | solution.py:76
  142.1 1.3 fusion.24
  143.4 0.0 copy-done.5
  143.4 11.4 %fusion = (f32[512]{0:T(512)S(1)}, f32[4096,512]{1,0:T(8,128)S(1)}) fusion(f32[4096]{0:T(1024)S(1)} %copy-done.5, f32[4096,512]{1,0:T(8,128)} %fusion.50, f32[130,512]{1,0:T(8,128)S(1)} %fusion.24, f32[128,4096]{1,0:T(8,128)S(1)} %get-tuple-element.123, f32[1,4096]{1,0:T(1,128)S(1)} %broadcast.33, f32[1,4096]{1,0:T(1,128)S(1)} %bitcast.47), kind=kOutput, calls=%fused_computation.16 | convolution fusion | flops 3285204480 | bytes 19191808 | tf_op jit(solution)/shard_map/dot_general | solution.py:80
  154.8 0.0 copy-start.1
  154.8 0.0 copy-start.6
  154.8 3.2 %copy-done.1 = f32[4096,512]{1,0:T(8,128)} copy-done((f32[4096,512]{1,0:T(8,128)}, f32[4096,512]{1,0:T(8,128)S(1)}, u32[]{:S(2)}) %copy-start.1) | copy-done | bytes 8388632
  158.0 1.8 exponential_reduce_fusion.3
  159.8 22.9 %all-gather.9 = f32[16,1,512]{2,1,0:T(1,128)S(1)} all-gather(f32[1,1,512]{2,1,0:T(1,128)S(1)} %bitcast.61), channel_id=3, replica_groups=mesh['src'=16,'tgt'=2] {'src'}, dimensions={0}, use_global_device_ids=true | all-gather | bytes 34816 | tf_op jit(solution)/shard_map/all_gather | solution.py:12
  182.7 17.5 %all-gather.8 = f32[16,1,512]{2,1,0:T(1,128)S(1)} all-gather(f32[1,1,512]{2,1,0:T(1,128)S(1)} %bitcast.58), channel_id=2, replica_groups=mesh['src'=16,'tgt'=2] {'src'}, dimensions={0}, use_global_device_ids=true | all-gather | bytes 34816 | tf_op jit(solution)/shard_map/all_gather | solution.py:12
  200.2 0.8 while.4
  201.0 0.0 copy-start.2
  201.0 0.0 copy-done.6
  201.0 0.0 copy-start.4
  201.1 4.4 %fusion.1 = f32[4096]{0:T(1024)S(1)} fusion(f32[4096,512]{1,0:T(8,128)} %copy-done.1, f32[512]{0:T(512)S(1)} %multiply_subtract_fusion.1), kind=kLoop, calls=%fused_computation.17 | loop fusion | flops 6287360 | bytes 8407040 | tf_op jit(solution)/shard_map/reduce_max | solution.py:44
  205.5 1.3 copy-done.2
  206.8 2.2 exponential_reduce_fusion.2
  209.0 4.4 %all-gather.2 = f32[8192]{0:T(1024)S(1)} all-gather(f32[4096]{0:T(1024)S(1)} %fusion.1), channel_id=4, replica_groups=mesh['src'=16,'tgt'=2] {'tgt'}, dimensions={0}, use_global_device_ids=true | all-gather | bytes 49152 | tf_op jit(solution)/shard_map/all_gather | solution.py:12
  213.4 4.4 %all-gather.3 = f32[8192]{0:T(1024)S(1)} all-gather(f32[4096]{0:T(1024)S(1)} %exponential_reduce_fusion.2), channel_id=5, replica_groups=mesh['src'=16,'tgt'=2] {'tgt'}, dimensions={0}, use_global_device_ids=true | all-gather | bytes 49152 | tf_op jit(solution)/shard_map/all_gather | solution.py:12
  217.8 0.0 copy-done.4
  217.8 1.0 fusion.2
  218.8 1.8 exponential_reduce_fusion.1
  220.6 18.9 %all-gather.11 = f32[16,1,512]{2,1,0:T(1,128)S(1)} all-gather(f32[1,1,512]{2,1,0:T(1,128)S(1)} %bitcast.60), channel_id=7, replica_groups=mesh['src'=16,'tgt'=2] {'src'}, dimensions={0}, use_global_device_ids=true | all-gather | bytes 34816 | tf_op jit(solution)/shard_map/all_gather | solution.py:12
  239.5 17.7 %all-gather.10 = f32[16,1,512]{2,1,0:T(1,128)S(1)} all-gather(f32[1,1,512]{2,1,0:T(1,128)S(1)} %bitcast.59), channel_id=6, replica_groups=mesh['src'=16,'tgt'=2] {'src'}, dimensions={0}, use_global_device_ids=true | all-gather | bytes 34816 | tf_op jit(solution)/shard_map/all_gather | solution.py:12
  257.2 0.8 while.5
  258.1 0.0 slice-start
  258.1 0.0 copy-start.7
  258.1 4.4 %fusion.3 = f32[4096]{0:T(1024)S(1)} fusion(f32[4096,512]{1,0:T(8,128)} %copy-done.1, f32[512]{0:T(512)S(1)} %multiply_subtract_fusion), kind=kLoop, calls=%fused_computation.19 | loop fusion | flops 6287360 | bytes 8407040 | tf_op jit(solution)/shard_map/reduce_max | solution.py:44
  262.5 0.0 slice-start.1
  262.5 5.1 %exponential_reduce_fusion = f32[4096]{0:T(1024)S(1)} fusion(f32[4096,512]{1,0:T(8,128)} %copy-done.1, f32[4096]{0:T(1024)S(1)} %fusion.3, f32[512]{0:T(512)S(1)} %multiply_subtract_fusion), kind=kLoop, calls=%fused_computation.7 | loop fusion | flops 8384512 | bytes 8423424 | tf_op jit(solution)/shard_map/reduce_sum | solution.py:45
  267.6 4.4 %all-gather.6 = f32[8192]{0:T(1024)S(1)} all-gather(f32[4096]{0:T(1024)S(1)} %fusion.3), channel_id=8, replica_groups=mesh['src'=16,'tgt'=2] {'tgt'}, dimensions={0}, use_global_device_ids=true | all-gather | bytes 49152 | tf_op jit(solution)/shard_map/all_gather | solution.py:12
  272.0 4.4 %all-gather.7 = f32[8192]{0:T(1024)S(1)} all-gather(f32[4096]{0:T(1024)S(1)} %exponential_reduce_fusion), channel_id=9, replica_groups=mesh['src'=16,'tgt'=2] {'tgt'}, dimensions={0}, use_global_device_ids=true | all-gather | bytes 49152 | tf_op jit(solution)/shard_map/all_gather | solution.py:12
  276.5 0.0 slice-done
  276.5 0.0 copy-done.7
  276.5 0.0 slice-done.1
  276.5 3.2 %convolution_convert_fusion = bf16[4096,256]{1,0:T(8,128)(2,1)} fusion(bf16[512,256]{1,0:T(8,128)(2,1)S(1)} %copy-done.7, f32[4096,512]{1,0:T(8,128)S(1)} %bitcast.41, f32[4096]{0:T(1024)S(1)} %fusion.36, f32[512]{0:T(512)S(1)} %multiply_subtract_fusion), kind=kOutput, calls=%fused_computation.20 | convolution fusion | flops 1083179008 | bytes 10766336 | tf_op jit(solution)/shard_map/dot_general | solution.py:109
  279.7 0.0 reduce-scatter.2.cloned.1.call-update
  279.8 30.3 %reduce-scatter.2.cloned.1.call-done = bf16[2048,256]{1,0:T(8,128)(2,1)} async-done(((bf16[4096,256]{1,0:T(8,128)(2,1)}), bf16[2048,256]{1,0:T(8,128)(2,1)}) %reduce-scatter.2.cloned.1.call-update) | async-done | bytes 1048592 | tf_op jit(solution)/shard_map/reduce_scatter | solution.py:108
  310.1 2.5 divide_convert_fusion
  (80 shorter events, 1.1 us)
Async XLA Ops:
  6.5 12.7 %copy-start = (bf16[128,4096]{1,0:T(8,128)(2,1)S(1)}, bf16[128,4096]{1,0:T(8,128)(2,1)}, u32[]{:S(2)}) copy-start(bf16[128,4096]{1,0:T(8,128)(2,1)} %param.15) | copy-start | bytes 3145732
  6.5 135.5 %all-reduce.2.cloned.1.call-start = ((), (), s32[]{:S(2)}) async-start(), calls=%async_computation.1 | async-start | bytes 278528 | tf_op jit(solution)/shard_map/psum | solution.py:76
  6.5 5.4 %copy-start.3 = (bf16[4096,512]{1,0:T(8,128)(2,1)S(1)}, bf16[4096,512]{1,0:T(8,128)(2,1)}, u32[]{:S(2)}) copy-start(bf16[4096,512]{1,0:T(8,128)(2,1)} %param.17) | copy-start | bytes 12582916
  19.0 124.4 %copy-start.5 = (f32[4096]{0:T(1024)S(1)}, f32[4096]{0:T(1024)}, u32[]{:S(2)}) copy-start(f32[4096]{0:T(1024)} %param.20) | copy-start | bytes 49156
  19.0 291.0 %reduce-scatter.2.cloned.1.call-start = ((), (), s32[]{:S(2)}) async-start(), calls=%async_computation.2 | async-start | bytes 3145728 | tf_op jit(solution)/shard_map/reduce_scatter | solution.py:108
  154.8 3.2 %copy-start.1 = (f32[4096,512]{1,0:T(8,128)}, f32[4096,512]{1,0:T(8,128)S(1)}, u32[]{:S(2)}) copy-start(f32[4096,512]{1,0:T(8,128)S(1)} %get-tuple-element.128) | copy-start | bytes 25165828
  154.8 46.2 %copy-start.6 = (f32[512]{0:T(512)S(1)}, f32[512]{0:T(512)}, u32[]{:S(2)}) copy-start(f32[512]{0:T(512)} %param.19) | copy-start | bytes 6148
  201.0 5.8 %copy-start.2 = (f32[4096,512]{1,0:T(8,128)S(1)}, f32[4096,512]{1,0:T(8,128)}, u32[]{:S(2)}) copy-start(f32[4096,512]{1,0:T(8,128)} %copy-done.1) | copy-start | bytes 25165828
  201.0 16.8 %copy-start.4 = (f32[4096]{0:T(1024)S(1)}, f32[4096]{0:T(1024)}, u32[]{:S(2)}) copy-start(f32[4096]{0:T(1024)} %param.18) | copy-start | bytes 49156
  258.1 18.4 %slice-start = ((s8[8388608]{0:T(1024)(128)(4,1)}), s8[4194304]{0:T(1024)(128)(4,1)S(1)}, s32[]{:S(2)}) async-start(s8[8388608]{0:T(1024)(128)(4,1)} %bitcast.40), calls=%async_computation.3 | async-start | bytes 8388608
  258.1 18.4 %copy-start.7 = (bf16[512,256]{1,0:T(8,128)(2,1)S(1)}, bf16[512,256]{1,0:T(8,128)(2,1)}, u32[]{:S(2)}) copy-start(bf16[512,256]{1,0:T(8,128)(2,1)} %param.21) | copy-start | bytes 786436
  262.5 14.0 %slice-start.1 = ((s8[8388608]{0:T(1024)(128)(4,1)}), s8[4194304]{0:T(1024)(128)(4,1)S(1)}, s32[]{:S(2)}) async-start(s8[8388608]{0:T(1024)(128)(4,1)} %bitcast.40), calls=%async_computation.4 | async-start | bytes 8388608
Sparse Core Ops, SparseCore 0:
  19.1 122.8 all-reduce.1
  279.9 30.1 reduce-scatter.1
where the time goes:
time: 320 us; the launch traced here: 319 us
  waiting for transfers between devices  148 us (46%)
  blocking collectives  94.5 us (30%)
  other arithmetic  29.3 us (9%)
  matrix products  28.4 us (9%)
  between operations  13.7 us (4%)
  local copies, waits for them, and re-layouts  4.93 us (2%)
    psum x1, waiting for transfers between devices, shards(): core_matrix = lax.psum(partial_core, ('src', 'tgt')) / total_pairs  117 us
    all_gather x8, blocking collectives, joined(): pieces = jax.tree.map(lambda part: lax.all_gather(part, axis), value)  94.5 us
    reduce_scatter x1, waiting for transfers between devices, shards(): lax.psum_scatter(jnp.dot(weights, target_genes, preferred_element_type=jn...  30.3 us
    dot_general x1, matrix products, shards(): lax.dot_general(left_src, geometry_right, (((0,), (0,)), ((), ())), preci...  11.4 us
    reduce_max x2, other arithmetic, row_logsum(): local_max = jnp.max(scores, axis=1)  8.87 us
    reduce_sum x2, other arithmetic, row_logsum(): local_sum = jnp.sum(jnp.exp(scores - local_max[:, None]), axis=1)  7.28 us
  transfers between devices with their start and end apart: 2, of which 2 were waited for; matrix products, arithmetic and copies ran while one was open for 2% of the time, Pallas kernels for 0%

commit v1 on v0

--- a/solution.py
+++ b/solution.py
@@ -73,7 +73,7 @@
     partial_core = jnp.dot(
         right_src, projected, precision=highest, preferred_element_type=jnp.float32
     )
-    core_matrix = lax.psum(partial_core, ("src", "tgt")) / total_pairs
+    core_matrix = lax.psum(lax.psum(partial_core, "tgt"), "src") / total_pairs
     geometry_right = jnp.dot(
         core_matrix, left_tgt, precision=highest, preferred_element_type=jnp.float32
     )

time: 320 us -> 311 us (0.972)
  waiting for transfers between devices: 148 us -> 140 us
    psum x1 -> x2, waiting for transfers between devices: 117 us -> 110 us  [shards(): core_matrix = lax.psum(lax.psum(partial_core, 'tgt'), 'src') / total_pairs]
  transfers between devices with their start and end apart: 2 -> 3, of which waited for: 2 -> 3; matrix products, arithmetic and copies ran while one was open for 2% -> 2% of each run, Pallas kernels for 0% -> 0%
where the time goes in v1:
time: 311 us; the launch traced here: 310 us
  waiting for transfers between devices  140 us (45%)
  blocking collectives  93.1 us (30%)
  other arithmetic  29.3 us (9%)
  matrix products  28.4 us (9%)
  between operations  13.4 us (4%)
  local copies, waits for them, and re-layouts  4.93 us (2%)
    psum x2, waiting for transfers between devices, shards(): core_matrix = lax.psum(lax.psum(partial_core, 'tgt'), 'src') / total_pairs  110 us
    all_gather x8, blocking collectives, joined(): pieces = jax.tree.map(lambda part: lax.all_gather(part, axis), value)  93.1 us
    reduce_scatter x1, waiting for transfers between devices, shards(): lax.psum_scatter(jnp.dot(weights, target_genes, preferred_element_type=jn...  30.3 us
    dot_general x1, matrix products, shards(): lax.dot_general(left_src, geometry_right, (((0,), (0,)), ((), ())), preci...  11.4 us
    reduce_max x2, other arithmetic, row_logsum(): local_max = jnp.max(scores, axis=1)  8.87 us
    reduce_sum x2, other arithmetic, row_logsum(): local_sum = jnp.sum(jnp.exp(scores - local_max[:, None]), axis=1)  7.28 us
  transfers between devices with their start and end apart: 3, of which 3 were waited for; matrix products, arithmetic and copies ran while one was open for 2% of the time, Pallas kernels for 0%

profile of v1, /device:TPU:0, one launch (start us, length us, event | category | flops | bytes accessed | tf_op | source)
XLA Modules:
  0.0 310.4 jit_solution(6774343998640118646)
XLA Ops:
  6.5 0.0 copy-start
  6.5 0.0 all-reduce.3.cloned.1.call-start
  6.5 0.0 copy-start.3
  6.5 1.1 multiply_reduce_fusion.1
  7.7 1.2 convert_element_type.20
  8.9 1.6 broadcast_multiply_fusion
  10.4 1.4 convert_element_type.19
  11.9 0.0 copy-done.3
  11.9 4.3 %fusion.18 = f32[130,4096]{1,0:T(8,128)S(1)} fusion(bf16[4096,512]{1,0:T(8,128)(2,1)S(1)} %copy-done.3, f32[128,512]{1,0:T(8,128)S(1)} %convert_element_type.20, f32[1,512]{1,0:T(1,128)S(1)} %bitcast.56, f32[1,512]{1,0:T(1,128)S(1)} %broadcast.34), kind=kOutput, calls=%fused_computation.38 | convolution fusion | flops 3271690240 | bytes 6590464 | tf_op jit(solution)/shard_map/dot_general | solution.py:67
  16.2 2.8 fusion.12
  19.0 0.0 copy-start.5
  19.0 0.0 all-reduce.3.cloned.1.call-update
  19.0 0.0 all-reduce.5.cloned.1.call-start
  19.1 24.4 %all-reduce.3.cloned.1.call-done = f32[130,130]{1,0:T(8,128)} async-done(((f32[130,130]{1,0:T(8,128)}), f32[130,130]{1,0:T(8,128)}) %all-reduce.3.cloned.1.call-update) | async-done | bytes 67616 | tf_op jit(solution)/shard_map/psum | solution.py:76
  43.4 0.0 all-reduce.5.cloned.1.call-update
  43.5 0.2 reduce-scatter.2.cloned.1.call-start
  43.7 0.0 copy-done
  43.7 5.4 %fusion.50 = f32[4096,512]{1,0:T(8,128)} fusion(bf16[128,4096]{1,0:T(8,128)(2,1)S(1)} %copy-done, bf16[128,512]{1,0:T(8,128)(2,1)} %param.16), kind=kOutput, calls=%fused_computation.86 | convolution fusion | flops 536870912 | bytes 9568256 | tf_op jit(solution)/shard_map/dot_general | solution.py:87
  49.1 85.6 %all-reduce.5.cloned.1.call-done = f32[130,130]{1,0:T(8,128)} async-done(((f32[130,130]{1,0:T(8,128)}), f32[130,130]{1,0:T(8,128)}) %all-reduce.5.cloned.1.call-update) | async-done | bytes 67616 | tf_op jit(solution)/shard_map/psum | solution.py:76
  134.7 1.3 fusion.24
  136.0 0.0 copy-done.5
  136.1 11.4 %fusion = (f32[512]{0:T(512)S(1)}, f32[4096,512]{1,0:T(8,128)S(1)}) fusion(f32[4096]{0:T(1024)S(1)} %copy-done.5, f32[4096,512]{1,0:T(8,128)} %fusion.50, f32[130,512]{1,0:T(8,128)S(1)} %fusion.24, f32[128,4096]{1,0:T(8,128)S(1)} %get-tuple-element.123, f32[1,4096]{1,0:T(1,128)S(1)} %broadcast.33, f32[1,4096]{1,0:T(1,128)S(1)} %bitcast.47), kind=kOutput, calls=%fused_computation.16 | convolution fusion | flops 3285204480 | bytes 19191808 | tf_op jit(solution)/shard_map/dot_general | solution.py:80
  147.4 0.0 copy-start.1
  147.4 0.0 copy-start.6
  147.5 3.2 %copy-done.1 = f32[4096,512]{1,0:T(8,128)} copy-done((f32[4096,512]{1,0:T(8,128)}, f32[4096,512]{1,0:T(8,128)S(1)}, u32[]{:S(2)}) %copy-start.1) | copy-done | bytes 8388632
  150.7 1.8 exponential_reduce_fusion.3
  152.5 21.4 %all-gather.9 = f32[16,1,512]{2,1,0:T(1,128)S(1)} all-gather(f32[1,1,512]{2,1,0:T(1,128)S(1)} %bitcast.61), channel_id=3, replica_groups=mesh['src'=16,'tgt'=2] {'src'}, dimensions={0}, use_global_device_ids=true | all-gather | bytes 34816 | tf_op jit(solution)/shard_map/all_gather | solution.py:12
  173.9 17.5 %all-gather.8 = f32[16,1,512]{2,1,0:T(1,128)S(1)} all-gather(f32[1,1,512]{2,1,0:T(1,128)S(1)} %bitcast.58), channel_id=2, replica_groups=mesh['src'=16,'tgt'=2] {'src'}, dimensions={0}, use_global_device_ids=true | all-gather | bytes 34816 | tf_op jit(solution)/shard_map/all_gather | solution.py:12
  191.4 0.8 while.4
  192.2 0.0 copy-start.2
  192.2 0.0 copy-done.6
  192.2 0.0 copy-start.4
  192.3 4.4 %fusion.1 = f32[4096]{0:T(1024)S(1)} fusion(f32[4096,512]{1,0:T(8,128)} %copy-done.1, f32[512]{0:T(512)S(1)} %multiply_subtract_fusion.1), kind=kLoop, calls=%fused_computation.17 | loop fusion | flops 6287360 | bytes 8407040 | tf_op jit(solution)/shard_map/reduce_max | solution.py:44
  196.7 1.3 copy-done.2
  198.0 2.2 exponential_reduce_fusion.2
  200.2 4.4 %all-gather.2 = f32[8192]{0:T(1024)S(1)} all-gather(f32[4096]{0:T(1024)S(1)} %fusion.1), channel_id=4, replica_groups=mesh['src'=16,'tgt'=2] {'tgt'}, dimensions={0}, use_global_device_ids=true | all-gather | bytes 49152 | tf_op jit(solution)/shard_map/all_gather | solution.py:12
  204.6 4.4 %all-gather.3 = f32[8192]{0:T(1024)S(1)} all-gather(f32[4096]{0:T(1024)S(1)} %exponential_reduce_fusion.2), channel_id=5, replica_groups=mesh['src'=16,'tgt'=2] {'tgt'}, dimensions={0}, use_global_device_ids=true | all-gather | bytes 49152 | tf_op jit(solution)/shard_map/all_gather | solution.py:12
  209.0 0.0 copy-done.4
  209.0 1.0 fusion.2
  210.0 1.8 exponential_reduce_fusion.1
  211.8 18.9 %all-gather.11 = f32[16,1,512]{2,1,0:T(1,128)S(1)} all-gather(f32[1,1,512]{2,1,0:T(1,128)S(1)} %bitcast.60), channel_id=7, replica_groups=mesh['src'=16,'tgt'=2] {'src'}, dimensions={0}, use_global_device_ids=true | all-gather | bytes 34816 | tf_op jit(solution)/shard_map/all_gather | solution.py:12
  230.7 17.7 %all-gather.10 = f32[16,1,512]{2,1,0:T(1,128)S(1)} all-gather(f32[1,1,512]{2,1,0:T(1,128)S(1)} %bitcast.59), channel_id=6, replica_groups=mesh['src'=16,'tgt'=2] {'src'}, dimensions={0}, use_global_device_ids=true | all-gather | bytes 34816 | tf_op jit(solution)/shard_map/all_gather | solution.py:12
  248.4 0.8 while.5
  249.2 0.0 slice-start
  249.3 0.0 copy-start.7
  249.3 4.4 %fusion.3 = f32[4096]{0:T(1024)S(1)} fusion(f32[4096,512]{1,0:T(8,128)} %copy-done.1, f32[512]{0:T(512)S(1)} %multiply_subtract_fusion), kind=kLoop, calls=%fused_computation.19 | loop fusion | flops 6287360 | bytes 8407040 | tf_op jit(solution)/shard_map/reduce_max | solution.py:44
  253.7 0.0 slice-start.1
  253.7 5.1 %exponential_reduce_fusion = f32[4096]{0:T(1024)S(1)} fusion(f32[4096,512]{1,0:T(8,128)} %copy-done.1, f32[4096]{0:T(1024)S(1)} %fusion.3, f32[512]{0:T(512)S(1)} %multiply_subtract_fusion), kind=kLoop, calls=%fused_computation.7 | loop fusion | flops 8384512 | bytes 8423424 | tf_op jit(solution)/shard_map/reduce_sum | solution.py:45
  258.8 4.4 %all-gather.6 = f32[8192]{0:T(1024)S(1)} all-gather(f32[4096]{0:T(1024)S(1)} %fusion.3), channel_id=8, replica_groups=mesh['src'=16,'tgt'=2] {'tgt'}, dimensions={0}, use_global_device_ids=true | all-gather | bytes 49152 | tf_op jit(solution)/shard_map/all_gather | solution.py:12
  263.2 4.4 %all-gather.7 = f32[8192]{0:T(1024)S(1)} all-gather(f32[4096]{0:T(1024)S(1)} %exponential_reduce_fusion), channel_id=9, replica_groups=mesh['src'=16,'tgt'=2] {'tgt'}, dimensions={0}, use_global_device_ids=true | all-gather | bytes 49152 | tf_op jit(solution)/shard_map/all_gather | solution.py:12
  267.7 0.0 slice-done
  267.7 0.0 copy-done.7
  267.7 0.0 slice-done.1
  267.7 3.2 %convolution_convert_fusion = bf16[4096,256]{1,0:T(8,128)(2,1)} fusion(bf16[512,256]{1,0:T(8,128)(2,1)S(1)} %copy-done.7, f32[4096,512]{1,0:T(8,128)S(1)} %bitcast.41, f32[4096]{0:T(1024)S(1)} %fusion.36, f32[512]{0:T(512)S(1)} %multiply_subtract_fusion), kind=kOutput, calls=%fused_computation.20 | convolution fusion | flops 1083179008 | bytes 10766336 | tf_op jit(solution)/shard_map/dot_general | solution.py:109
  270.9 0.0 reduce-scatter.2.cloned.1.call-update
  271.0 30.3 %reduce-scatter.2.cloned.1.call-done = bf16[2048,256]{1,0:T(8,128)(2,1)} async-done(((bf16[4096,256]{1,0:T(8,128)(2,1)}), bf16[2048,256]{1,0:T(8,128)(2,1)}) %reduce-scatter.2.cloned.1.call-update) | async-done | bytes 1048592 | tf_op jit(solution)/shard_map/reduce_scatter | solution.py:108
  301.3 2.5 divide_convert_fusion
  (80 shorter events, 1.1 us)
Async XLA Ops:
  6.5 37.2 %copy-start = (bf16[128,4096]{1,0:T(8,128)(2,1)S(1)}, bf16[128,4096]{1,0:T(8,128)(2,1)}, u32[]{:S(2)}) copy-start(bf16[128,4096]{1,0:T(8,128)(2,1)} %param.15) | copy-start | bytes 3145732
  6.5 36.9 %all-reduce.3.cloned.1.call-start = ((), (), s32[]{:S(2)}) async-start(), calls=%async_computation.1 | async-start | bytes 278528 | tf_op jit(solution)/shard_map/psum | solution.py:76
  6.5 5.4 %copy-start.3 = (bf16[4096,512]{1,0:T(8,128)(2,1)S(1)}, bf16[4096,512]{1,0:T(8,128)(2,1)}, u32[]{:S(2)}) copy-start(bf16[4096,512]{1,0:T(8,128)(2,1)} %param.17) | copy-start | bytes 12582916
  19.0 117.0 %copy-start.5 = (f32[4096]{0:T(1024)S(1)}, f32[4096]{0:T(1024)}, u32[]{:S(2)}) copy-start(f32[4096]{0:T(1024)} %param.20) | copy-start | bytes 49156
  19.0 115.7 %all-reduce.5.cloned.1.call-start = ((), (), s32[]{:S(2)}) async-start(), calls=%async_computation.2 | async-start | bytes 278528 | tf_op jit(solution)/shard_map/psum | solution.py:76
  43.5 257.8 %reduce-scatter.2.cloned.1.call-start = ((), (), s32[]{:S(2)}) async-start(), calls=%async_computation.3 | async-start | bytes 3145728 | tf_op jit(solution)/shard_map/reduce_scatter | solution.py:108
  147.4 3.2 %copy-start.1 = (f32[4096,512]{1,0:T(8,128)}, f32[4096,512]{1,0:T(8,128)S(1)}, u32[]{:S(2)}) copy-start(f32[4096,512]{1,0:T(8,128)S(1)} %get-tuple-element.128) | copy-start | bytes 25165828
  147.4 44.8 %copy-start.6 = (f32[512]{0:T(512)S(1)}, f32[512]{0:T(512)}, u32[]{:S(2)}) copy-start(f32[512]{0:T(512)} %param.19) | copy-start | bytes 6148
  192.2 5.8 %copy-start.2 = (f32[4096,512]{1,0:T(8,128)S(1)}, f32[4096,512]{1,0:T(8,128)}, u32[]{:S(2)}) copy-start(f32[4096,512]{1,0:T(8,128)} %copy-done.1) | copy-start | bytes 25165828
  192.2 16.8 %copy-start.4 = (f32[4096]{0:T(1024)S(1)}, f32[4096]{0:T(1024)}, u32[]{:S(2)}) copy-start(f32[4096]{0:T(1024)} %param.18) | copy-start | bytes 49156
  249.2 18.4 %slice-start = ((s8[8388608]{0:T(1024)(128)(4,1)}), s8[4194304]{0:T(1024)(128)(4,1)S(1)}, s32[]{:S(2)}) async-start(s8[8388608]{0:T(1024)(128)(4,1)} %bitcast.40), calls=%async_computation.4 | async-start | bytes 8388608
  249.3 18.4 %copy-start.7 = (bf16[512,256]{1,0:T(8,128)(2,1)S(1)}, bf16[512,256]{1,0:T(8,128)(2,1)}, u32[]{:S(2)}) copy-start(bf16[512,256]{1,0:T(8,128)(2,1)} %param.21) | copy-start | bytes 786436
  253.7 14.0 %slice-start.1 = ((s8[8388608]{0:T(1024)(128)(4,1)}), s8[4194304]{0:T(1024)(128)(4,1)S(1)}, s32[]{:S(2)}) async-start(s8[8388608]{0:T(1024)(128)(4,1)} %bitcast.40), calls=%async_computation.5 | async-start | bytes 8388608
Sparse Core Ops, SparseCore 0:
  19.1 24.2 all-reduce.2
  46.9 87.7 all-reduce.4
  271.1 30.1 reduce-scatter.1
